TPU v7x, 32 devices: a whole 2x2x4 slice. The times are simulated.
32 devices in a mesh: sector: 8 (over z, y), mpo: 4 (over x, core).
Axes of the slice: x: 2, y: 2, z: 4, core: 2. Of those that a mesh axis runs over, the one named last changes fastest.
Arguments:
- vectors: bfloat16 [16, 8, 256, 256], P(None, 'sector'), may hold values from -6 to 6
- left_env: bfloat16 [16, 8, 256, 256], P('mpo', 'sector'), may hold values from -4 to 4
- right_env: bfloat16 [16, 8, 256, 256], P('mpo', 'sector'), may hold values from -4 to 4
- bond_shift: int32 [16], replicated, may hold values from -1 to 1, as said below
Outputs:
- sigma: bfloat16 [16, 8, 256, 256], P('mpo', 'sector')
- intersection: float32 [16, 16], replicated
- ham_small: float32 [16, 16], replicated
Inputs may be any that keep to these rules, and one draw needn't show every extreme that they name: `bond_shift`: every one of -1, 0 and 1 occurs.
All inputs are finite; a program needn't handle non-finite values.
Results may differ from a plain program's by a relative error of at most 0.0034.
Values may be sent and summed in bfloat16 or wider, within the bound.
A program may use at most 128 MiB of HBM per device.

v0:
```python
import jax
import jax.numpy as jnp
from jax import lax
from jax.sharding import PartitionSpec as P


def with_halo(cells, sides, width):
    for axis, dim in sides:
        count = lax.axis_size(axis)
        ends = count - 1
        head = lax.slice_in_dim(cells, 0, width, axis=dim)
        tail = lax.slice_in_dim(cells, cells.shape[dim] - width, cells.shape[dim], axis=dim)
        cells = jnp.concatenate(
            [
                lax.ppermute(tail, axis, [(i, (i + 1) % count) for i in range(ends)]),
                cells,
                lax.ppermute(head, axis, [((i + 1) % count, i) for i in range(ends)]),
            ],
            axis=dim,
        )
    return cells


def bond_term(extended, lenv, renv, shift):
    source = lax.dynamic_slice_in_dim(extended, 1 + shift, lenv.shape[0], 1)
    left = jnp.einsum("sab,vsbc->vsac", lenv, source, preferred_element_type=jnp.float32).astype(
        jnp.bfloat16
    )
    return jnp.einsum("vsac,scd->vsad", left, renv, preferred_element_type=jnp.float32)


def body(vectors, left_env, right_env, bond_shift):
    group = lax.axis_size("mpo")
    per_owner = vectors.shape[0] // group
    owner_start = lax.axis_index("mpo") * per_owner
    owned = lax.dynamic_slice_in_dim(vectors, owner_start, per_owner, 0)
    extended = with_halo(owned, (("sector", 1),), 1)
    empty = jnp.zeros(owned.shape, jnp.float32)
    lpiece = lax.all_gather(left_env, "mpo", axis=0, tiled=True)
    rpiece = lax.all_gather(right_env, "mpo", axis=0, tiled=True)

    def step(index, accum):
        shift = lax.dynamic_index_in_dim(bond_shift, index, 0, keepdims=False)
        return accum + bond_term(extended, lpiece[index], rpiece[index], shift)

    summed = lax.fori_loop(0, lpiece.shape[0], step, empty)
    sigma = summed.astype(jnp.bfloat16)
    scale = 1.0 / (lax.axis_size("sector") * vectors.shape[1] * vectors.shape[2] * vectors.shape[3])
    zeros_small = jnp.zeros((vectors.shape[0], vectors.shape[0]), jnp.float32)
    ham_cols = jnp.einsum("isab,jsab->ij", vectors, sigma, preferred_element_type=jnp.float32)
    ham_part = lax.dynamic_update_slice(zeros_small, ham_cols, (jnp.int32(0), owner_start))
    full_intersection = jnp.einsum(
        "isab,jsab->ij", vectors, vectors, preferred_element_type=jnp.float32
    )
    intersection = lax.psum(full_intersection, "sector")
    ham_small = lax.psum(ham_part, ("sector", "mpo"))
    return (sigma, intersection * scale, ham_small * scale)


def solution(mesh):
    return jax.shard_map(
        body,
        mesh=mesh,
        in_specs=(
            P(None, "sector", None, None),
            P("mpo", "sector", None, None),
            P("mpo", "sector", None, None),
            P(),
        ),
        out_specs=(P("mpo", "sector", None, None), P(), P()),
        check_vma=False,
    )
```

profile of v0, /device:TPU:0, one launch (start us, length us, event | category | flops | bytes accessed | tf_op | source)
XLA Modules:
  0.0 170.0 jit_solution(12909830077423487255)
XLA Ops:
  7.2 0.7 all-gather.3.cloned.1.call-update
  7.9 0.7 all-gather.5.cloned.1.call-update
  8.7 1.1 constant_dynamic-slice_fusion
  9.9 4.9 %collective-permute-start = (bf16[4,1,256,256]{2,3,0,1:T(8,128)(2,1)S(1)}, bf16[4,1,256,256]{2,3,0,1:T(8,128)(2,1)S(1)}, u32[]{:S(2)}, u32[]{:S(2)}) collective-permute-start(bf16[4,1,256,256]{2,3,0,1:T(8,128)(2,1)S(1)} %copy.29), channel_id=1, source_target_pairs={{0,4},{4,8},{8,12},{12,16},{16,20},{20,24},{24,28},{1,5},{5,9},{9,... | collective-permute-start | bytes 1572872 | tf_op jit(solution)/shard_map/ppermute | solution.py:15
  14.9 1.3 collective-permute-start.1
  16.2 4.9 %fusion.18 = f32[16,16]{1,0:T(8,128)S(1)} fusion(bf16[16,256,256]{2,1,0:T(8,128)(2,1)} %bitcast.55), kind=kOutput, calls=%fused_computation.16 | convolution fusion | flops 33554432 | bytes 2098176 | tf_op jit(solution)/shard_map/isab,jsab->ij/dot_general | solution.py:52
  21.1 29.0 %psum.14 = f32[16,16]{1,0:T(8,128)S(1)} all-reduce(f32[16,16]{1,0:T(8,128)S(1)} %fusion.18), channel_id=1, replica_groups=mesh['sector'=8,'mpo'=4] {'sector'}, use_global_device_ids=true, to_apply=%region_2.3 | all-reduce | flops 256 | bytes 2048 | tf_op jit(solution)/shard_map/psum | solution.py:55
  50.0 0.6 broadcast_multiply_fusion.1
  50.6 0.8 copy-done.1
  51.4 1.4 pad_maximum_fusion
  52.8 6.2 %all-gather.5.cloned.1.call-done = bf16[16,1,256,256]{3,2,1,0:T(8,128)(2,1)} async-done(((bf16[4,1,256,256]{3,2,1,0:T(8,128)(2,1)}), bf16[16,1,256,256]{3,2,1,0:T(8,128)(2,1)}) %all-gather.5.cloned.1.call-update) | async-done | bytes 2097168 | tf_op jit(solution)/shard_map/all_gather | solution.py:39
  59.0 60.5 %while.16 = (s32[]{:T(128)}, f32[4,1,256,256]{2,3,0,1:T(8,128)S(1)}, bf16[16,1,256,256]{3,2,1,0:T(8,128)(2,1)}, s32[16]{0:T(128)S(1)}, bf16[4,3,256,256]{2,3,0,1...) while((s32[]{:T(128)}, ...), condition=%wide.region_1.2_spmd.clone, body=%wide.region_0.1_spmd.clone.sunk | while | flops 269221888 | bytes 2884781 | solution.py:46
  60.9 1.9 %fusion.32 = f32[4,1,256,256]{2,3,0,1:T(8,128)S(1)} fusion(f32[4,1,256,256]{2,3,0,1:T(8,128)S(1)} %get-tuple-element.245, bf16[4,3,256,256]{2,3,0,1:T(8,128)(2,1)S(1)} %get-tuple-element.258, s32[]{:T(128)S(6)} %select_n.28, pred[]{:T(512)S(6)} %compare.3, bf16[16,1,256,256]{3,2,1,0:T(8,128)(2,1)} %get-tuple-element.259, s32[]{:T(128)} %get-tuple-element.244, ...), kind=kOutput, calls=%fused_computation.1.clone.1 | convolution fusion | flops 269221888 | bytes 2884613 | tf_op jit(solution)/shard_map/while/body/eval_jaxpr/vsac,scd->vsad/dot_general | solution.py:29
  62.8 0.6 dynamic_slice.71
  64.7 1.9 %fusion.32 = f32[4,1,256,256]{2,3,0,1:T(8,128)S(1)} fusion(f32[4,1,256,256]{2,3,0,1:T(8,128)S(1)} %get-tuple-element.245, bf16[4,3,256,256]{2,3,0,1:T(8,128)(2,1)S(1)} %get-tuple-element.258, s32[]{:T(128)S(6)} %select_n.28, pred[]{:T(512)S(6)} %compare.3, bf16[16,1,256,256]{3,2,1,0:T(8,128)(2,1)} %get-tuple-element.259, s32[]{:T(128)} %get-tuple-element.244, ...), kind=kOutput, calls=%fused_computation.1.clone.1 | convolution fusion | flops 269221888 | bytes 2884613 | tf_op jit(solution)/shard_map/while/body/eval_jaxpr/vsac,scd->vsad/dot_general | solution.py:29
  68.5 1.9 %fusion.32 = f32[4,1,256,256]{2,3,0,1:T(8,128)S(1)} fusion(f32[4,1,256,256]{2,3,0,1:T(8,128)S(1)} %get-tuple-element.245, bf16[4,3,256,256]{2,3,0,1:T(8,128)(2,1)S(1)} %get-tuple-element.258, s32[]{:T(128)S(6)} %select_n.28, pred[]{:T(512)S(6)} %compare.3, bf16[16,1,256,256]{3,2,1,0:T(8,128)(2,1)} %get-tuple-element.259, s32[]{:T(128)} %get-tuple-element.244, ...), kind=kOutput, calls=%fused_computation.1.clone.1 | convolution fusion | flops 269221888 | bytes 2884613 | tf_op jit(solution)/shard_map/while/body/eval_jaxpr/vsac,scd->vsad/dot_general | solution.py:29
  72.2 1.9 %fusion.32 = f32[4,1,256,256]{2,3,0,1:T(8,128)S(1)} fusion(f32[4,1,256,256]{2,3,0,1:T(8,128)S(1)} %get-tuple-element.245, bf16[4,3,256,256]{2,3,0,1:T(8,128)(2,1)S(1)} %get-tuple-element.258, s32[]{:T(128)S(6)} %select_n.28, pred[]{:T(512)S(6)} %compare.3, bf16[16,1,256,256]{3,2,1,0:T(8,128)(2,1)} %get-tuple-element.259, s32[]{:T(128)} %get-tuple-element.244, ...), kind=kOutput, calls=%fused_computation.1.clone.1 | convolution fusion | flops 269221888 | bytes 2884613 | tf_op jit(solution)/shard_map/while/body/eval_jaxpr/vsac,scd->vsad/dot_general | solution.py:29
  76.0 1.9 %fusion.32 = f32[4,1,256,256]{2,3,0,1:T(8,128)S(1)} fusion(f32[4,1,256,256]{2,3,0,1:T(8,128)S(1)} %get-tuple-element.245, bf16[4,3,256,256]{2,3,0,1:T(8,128)(2,1)S(1)} %get-tuple-element.258, s32[]{:T(128)S(6)} %select_n.28, pred[]{:T(512)S(6)} %compare.3, bf16[16,1,256,256]{3,2,1,0:T(8,128)(2,1)} %get-tuple-element.259, s32[]{:T(128)} %get-tuple-element.244, ...), kind=kOutput, calls=%fused_computation.1.clone.1 | convolution fusion | flops 269221888 | bytes 2884613 | tf_op jit(solution)/shard_map/while/body/eval_jaxpr/vsac,scd->vsad/dot_general | solution.py:29
  79.8 1.9 %fusion.32 = f32[4,1,256,256]{2,3,0,1:T(8,128)S(1)} fusion(f32[4,1,256,256]{2,3,0,1:T(8,128)S(1)} %get-tuple-element.245, bf16[4,3,256,256]{2,3,0,1:T(8,128)(2,1)S(1)} %get-tuple-element.258, s32[]{:T(128)S(6)} %select_n.28, pred[]{:T(512)S(6)} %compare.3, bf16[16,1,256,256]{3,2,1,0:T(8,128)(2,1)} %get-tuple-element.259, s32[]{:T(128)} %get-tuple-element.244, ...), kind=kOutput, calls=%fused_computation.1.clone.1 | convolution fusion | flops 269221888 | bytes 2884613 | tf_op jit(solution)/shard_map/while/body/eval_jaxpr/vsac,scd->vsad/dot_general | solution.py:29
  83.6 1.9 %fusion.32 = f32[4,1,256,256]{2,3,0,1:T(8,128)S(1)} fusion(f32[4,1,256,256]{2,3,0,1:T(8,128)S(1)} %get-tuple-element.245, bf16[4,3,256,256]{2,3,0,1:T(8,128)(2,1)S(1)} %get-tuple-element.258, s32[]{:T(128)S(6)} %select_n.28, pred[]{:T(512)S(6)} %compare.3, bf16[16,1,256,256]{3,2,1,0:T(8,128)(2,1)} %get-tuple-element.259, s32[]{:T(128)} %get-tuple-element.244, ...), kind=kOutput, calls=%fused_computation.1.clone.1 | convolution fusion | flops 269221888 | bytes 2884613 | tf_op jit(solution)/shard_map/while/body/eval_jaxpr/vsac,scd->vsad/dot_general | solution.py:29
  87.4 1.9 %fusion.32 = f32[4,1,256,256]{2,3,0,1:T(8,128)S(1)} fusion(f32[4,1,256,256]{2,3,0,1:T(8,128)S(1)} %get-tuple-element.245, bf16[4,3,256,256]{2,3,0,1:T(8,128)(2,1)S(1)} %get-tuple-element.258, s32[]{:T(128)S(6)} %select_n.28, pred[]{:T(512)S(6)} %compare.3, bf16[16,1,256,256]{3,2,1,0:T(8,128)(2,1)} %get-tuple-element.259, s32[]{:T(128)} %get-tuple-element.244, ...), kind=kOutput, calls=%fused_computation.1.clone.1 | convolution fusion | flops 269221888 | bytes 2884613 | tf_op jit(solution)/shard_map/while/body/eval_jaxpr/vsac,scd->vsad/dot_general | solution.py:29
  91.1 1.9 %fusion.32 = f32[4,1,256,256]{2,3,0,1:T(8,128)S(1)} fusion(f32[4,1,256,256]{2,3,0,1:T(8,128)S(1)} %get-tuple-element.245, bf16[4,3,256,256]{2,3,0,1:T(8,128)(2,1)S(1)} %get-tuple-element.258, s32[]{:T(128)S(6)} %select_n.28, pred[]{:T(512)S(6)} %compare.3, bf16[16,1,256,256]{3,2,1,0:T(8,128)(2,1)} %get-tuple-element.259, s32[]{:T(128)} %get-tuple-element.244, ...), kind=kOutput, calls=%fused_computation.1.clone.1 | convolution fusion | flops 269221888 | bytes 2884613 | tf_op jit(solution)/shard_map/while/body/eval_jaxpr/vsac,scd->vsad/dot_general | solution.py:29
  94.9 1.9 %fusion.32 = f32[4,1,256,256]{2,3,0,1:T(8,128)S(1)} fusion(f32[4,1,256,256]{2,3,0,1:T(8,128)S(1)} %get-tuple-element.245, bf16[4,3,256,256]{2,3,0,1:T(8,128)(2,1)S(1)} %get-tuple-element.258, s32[]{:T(128)S(6)} %select_n.28, pred[]{:T(512)S(6)} %compare.3, bf16[16,1,256,256]{3,2,1,0:T(8,128)(2,1)} %get-tuple-element.259, s32[]{:T(128)} %get-tuple-element.244, ...), kind=kOutput, calls=%fused_computation.1.clone.1 | convolution fusion | flops 269221888 | bytes 2884613 | tf_op jit(solution)/shard_map/while/body/eval_jaxpr/vsac,scd->vsad/dot_general | solution.py:29
  98.7 1.9 %fusion.32 = f32[4,1,256,256]{2,3,0,1:T(8,128)S(1)} fusion(f32[4,1,256,256]{2,3,0,1:T(8,128)S(1)} %get-tuple-element.245, bf16[4,3,256,256]{2,3,0,1:T(8,128)(2,1)S(1)} %get-tuple-element.258, s32[]{:T(128)S(6)} %select_n.28, pred[]{:T(512)S(6)} %compare.3, bf16[16,1,256,256]{3,2,1,0:T(8,128)(2,1)} %get-tuple-element.259, s32[]{:T(128)} %get-tuple-element.244, ...), kind=kOutput, calls=%fused_computation.1.clone.1 | convolution fusion | flops 269221888 | bytes 2884613 | tf_op jit(solution)/shard_map/while/body/eval_jaxpr/vsac,scd->vsad/dot_general | solution.py:29
  102.5 1.9 %fusion.32 = f32[4,1,256,256]{2,3,0,1:T(8,128)S(1)} fusion(f32[4,1,256,256]{2,3,0,1:T(8,128)S(1)} %get-tuple-element.245, bf16[4,3,256,256]{2,3,0,1:T(8,128)(2,1)S(1)} %get-tuple-element.258, s32[]{:T(128)S(6)} %select_n.28, pred[]{:T(512)S(6)} %compare.3, bf16[16,1,256,256]{3,2,1,0:T(8,128)(2,1)} %get-tuple-element.259, s32[]{:T(128)} %get-tuple-element.244, ...), kind=kOutput, calls=%fused_computation.1.clone.1 | convolution fusion | flops 269221888 | bytes 2884613 | tf_op jit(solution)/shard_map/while/body/eval_jaxpr/vsac,scd->vsad/dot_general | solution.py:29
  106.3 1.9 %fusion.32 = f32[4,1,256,256]{2,3,0,1:T(8,128)S(1)} fusion(f32[4,1,256,256]{2,3,0,1:T(8,128)S(1)} %get-tuple-element.245, bf16[4,3,256,256]{2,3,0,1:T(8,128)(2,1)S(1)} %get-tuple-element.258, s32[]{:T(128)S(6)} %select_n.28, pred[]{:T(512)S(6)} %compare.3, bf16[16,1,256,256]{3,2,1,0:T(8,128)(2,1)} %get-tuple-element.259, s32[]{:T(128)} %get-tuple-element.244, ...), kind=kOutput, calls=%fused_computation.1.clone.1 | convolution fusion | flops 269221888 | bytes 2884613 | tf_op jit(solution)/shard_map/while/body/eval_jaxpr/vsac,scd->vsad/dot_general | solution.py:29
  110.0 1.9 %fusion.32 = f32[4,1,256,256]{2,3,0,1:T(8,128)S(1)} fusion(f32[4,1,256,256]{2,3,0,1:T(8,128)S(1)} %get-tuple-element.245, bf16[4,3,256,256]{2,3,0,1:T(8,128)(2,1)S(1)} %get-tuple-element.258, s32[]{:T(128)S(6)} %select_n.28, pred[]{:T(512)S(6)} %compare.3, bf16[16,1,256,256]{3,2,1,0:T(8,128)(2,1)} %get-tuple-element.259, s32[]{:T(128)} %get-tuple-element.244, ...), kind=kOutput, calls=%fused_computation.1.clone.1 | convolution fusion | flops 269221888 | bytes 2884613 | tf_op jit(solution)/shard_map/while/body/eval_jaxpr/vsac,scd->vsad/dot_general | solution.py:29
  113.8 1.9 %fusion.32 = f32[4,1,256,256]{2,3,0,1:T(8,128)S(1)} fusion(f32[4,1,256,256]{2,3,0,1:T(8,128)S(1)} %get-tuple-element.245, bf16[4,3,256,256]{2,3,0,1:T(8,128)(2,1)S(1)} %get-tuple-element.258, s32[]{:T(128)S(6)} %select_n.28, pred[]{:T(512)S(6)} %compare.3, bf16[16,1,256,256]{3,2,1,0:T(8,128)(2,1)} %get-tuple-element.259, s32[]{:T(128)} %get-tuple-element.244, ...), kind=kOutput, calls=%fused_computation.1.clone.1 | convolution fusion | flops 269221888 | bytes 2884613 | tf_op jit(solution)/shard_map/while/body/eval_jaxpr/vsac,scd->vsad/dot_general | solution.py:29
  117.6 1.9 %fusion.32 = f32[4,1,256,256]{2,3,0,1:T(8,128)S(1)} fusion(f32[4,1,256,256]{2,3,0,1:T(8,128)S(1)} %get-tuple-element.245, bf16[4,3,256,256]{2,3,0,1:T(8,128)(2,1)S(1)} %get-tuple-element.258, s32[]{:T(128)S(6)} %select_n.28, pred[]{:T(512)S(6)} %compare.3, bf16[16,1,256,256]{3,2,1,0:T(8,128)(2,1)} %get-tuple-element.259, s32[]{:T(128)} %get-tuple-element.244, ...), kind=kOutput, calls=%fused_computation.1.clone.1 | convolution fusion | flops 269221888 | bytes 2884613 | tf_op jit(solution)/shard_map/while/body/eval_jaxpr/vsac,scd->vsad/dot_general | solution.py:29
  119.7 3.3 %fusion.21 = f32[16,4]{1,0:T(8,128)S(1)} fusion(bf16[16,256,256]{2,1,0:T(8,128)(2,1)} %bitcast.56, bf16[4,256,256]{2,1,0:T(8,128)(2,1)S(1)} %bitcast.54), kind=kOutput, calls=%fused_computation.17 | convolution fusion | flops 8388608 | bytes 2621696 | tf_op jit(solution)/shard_map/isab,jsab->ij/dot_general | solution.py:50
  123.2 39.4 %psum.15 = f32[16,16]{1,0:T(8,128)S(1)} all-reduce(f32[16,16]{1,0:T(8,128)S(1)} %dynamic_update_slice.3), channel_id=1, replica_groups=mesh['sector'=8,'mpo'=4] {'sector','mpo'}, use_global_device_ids=true, to_apply=%region_3.4 | all-reduce | flops 256 | bytes 2048 | tf_op jit(solution)/shard_map/psum | solution.py:56
  162.6 0.6 broadcast_multiply_fusion
  (30 shorter events, 9.5 us)
Async XLA Ops:
  7.2 45.7 %all-gather.3.cloned.1.call-start = ((), (), s32[]{:S(2)}) async-start(), calls=%async_computation | async-start | bytes 2621440 | tf_op jit(solution)/shard_map/all_gather | solution.py:40
  7.9 51.1 %all-gather.5.cloned.1.call-start = ((), (), s32[]{:S(2)}) async-start(), calls=%async_computation.1 | async-start | bytes 2621440 | tf_op jit(solution)/shard_map/all_gather | solution.py:39
  9.9 40.7 %collective-permute-start = (bf16[4,1,256,256]{2,3,0,1:T(8,128)(2,1)S(1)}, bf16[4,1,256,256]{2,3,0,1:T(8,128)(2,1)S(1)}, u32[]{:S(2)}, u32[]{:S(2)}) collective-permute-start(bf16[4,1,256,256]{2,3,0,1:T(8,128)(2,1)S(1)} %copy.29), channel_id=1, source_target_pairs={{0,4},{4,8},{8,12},{12,16},{16,20},{20,24},{24,28},{1,5},{5,9},{9,... | collective-permute-start | bytes 1572872 | tf_op jit(solution)/shard_map/ppermute | solution.py:15
  14.9 36.5 %collective-permute-start.1 = (bf16[4,1,256,256]{2,3,0,1:T(8,128)(2,1)S(1)}, bf16[4,1,256,256]{2,3,0,1:T(8,128)(2,1)}, u32[]{:S(2)}, u32[]{:S(2)}) collective-permute-start(bf16[4,1,256,256]{2,3,0,1:T(8,128)(2,1)S(1)} %copy.29), channel_id=1, source_target_pairs={{4,0},{8,4},{12,8},{16,12},{20,16},{24,20},{28,24},{5,1},{9,5},{13... | collective-permute-start | bytes 1572872 | tf_op jit(solution)/shard_map/ppermute | solution.py:17
  21.1 38.0 %copy-start.2 = (s32[16]{0:T(128)S(1)}, s32[16]{0:T(128)}, u32[]{:S(2)}) copy-start(s32[16]{0:T(128)} %param.9) | copy-start | bytes 196
  50.6 0.8 copy-start.1
  119.7 3.3 %copy-start = (bf16[4,1,256,256]{3,2,1,0:T(8,128)(2,1)}, bf16[4,1,256,256]{3,2,1,0:T(8,128)(2,1)S(1)}, u32[]{:S(2)}) copy-start(bf16[4,1,256,256]{3,2,1,0:T(8,128)(2,1)S(1)} %copy.19) | copy-start | bytes 1572868
Sparse Core Ops, SparseCore 0:
  9.5 25.2 all-gather.2
  36.4 22.5 all-gather.4
where the time goes:
time: 171 us; the launch traced here: 170 us
  blocking collectives  68.3 us (40%)
  matrix products  38 us (22%)
  loops' own time  21.2 us (12%)
  between operations  14.1 us (8%)
  local copies, waits for them, and re-layouts  11.9 us (7%)
  waiting for transfers between devices  7.58 us (4%)
  starting transfers between devices  6.3 us (4%)
  other arithmetic  2.58 us (2%)
    psum x1, blocking collectives, body(): ham_small = lax.psum(ham_part, ('sector', 'mpo'))  39.4 us
    dot_general x16, matrix products, bond_term(): jnp.einsum('vsac,scd->vsad', left, renv, preferred_element_type=jnp.float32)  29.9 us
    psum x1, blocking collectives, body(): intersection = lax.psum(full_intersection, 'sector')  29 us
    another operation x1, loops' own time, body(): summed = lax.fori_loop(0, lpiece.shape[0], step, empty)  21.2 us
    dynamic_slice x16, local copies, waits for them, and re-layouts, step(): shift = lax.dynamic_index_in_dim(bond_shift, index, 0, keepdims=False)  9.38 us
    all_gather x1, waiting for transfers between devices, body(): lpiece = lax.all_gather(left_env, 'mpo', axis=0, tiled=True)  6.17 us
    ppermute x1, starting transfers between devices, with_halo(): lax.ppermute(tail, axis, [(i, (i + 1) % count) for i in range(ends)])  4.93 us
    dot_general x1, matrix products, body(): jnp.einsum('isab,jsab->ij', vectors, vectors, preferred_element_type=jnp....  4.86 us
  transfers between devices with their start and end apart: 4, of which 1 were waited for; matrix products, arithmetic and copies ran while one was open for 5% of the time, Pallas kernels for 0%

commit v1 on v0

--- a/solution.py
+++ b/solution.py
@@ -52,7 +52,7 @@
     full_intersection = jnp.einsum(
         "isab,jsab->ij", vectors, vectors, preferred_element_type=jnp.float32
     )
-    intersection = lax.psum(full_intersection, "sector")
+    intersection = jnp.sum(lax.all_gather(full_intersection, "sector"), axis=0)
     ham_small = lax.psum(ham_part, ("sector", "mpo"))
     return (sigma, intersection * scale, ham_small * scale)
 

time: 171 us -> 177 us (1.035)
  blocking collectives: 68.3 us -> 79.2 us
  waiting for transfers between devices: 7.58 us -> 1.42 us
    all_gather x0 -> x1, blocking collectives: none -> 42.3 us  [body(): intersection = jnp.sum(lax.all_gather(full_intersection, 'sector'), axis=0)]
    psum x1 -> x0, blocking collectives: 29 us -> none  [body(): intersection = lax.psum(full_intersection, 'sector')]
    all_gather x1, waiting for transfers between devices: 6.17 us -> 0.02 us  [body(): lpiece = lax.all_gather(left_env, 'mpo', axis=0, tiled=True)]
    psum x1, blocking collectives: 39.4 us -> 36.9 us  [body(): ham_small = lax.psum(ham_part, ('sector', 'mpo'))]
  transfers between devices with their start and end apart: 4 -> 4, of which waited for: 1 -> 0; matrix products, arithmetic and copies ran while one was open for 5% -> 5% of each run, Pallas kernels for 0% -> 0%
where the time goes in v1:
time: 177 us; the launch traced here: 175 us
  blocking collectives  79.2 us (45%)
  matrix products  38.3 us (22%)
  loops' own time  21.2 us (12%)
  between operations  14.1 us (8%)
  local copies, waits for them, and re-layouts  11.9 us (7%)
  starting transfers between devices  6.3 us (4%)
  other arithmetic  2.59 us (1%)
    all_gather x1, blocking collectives, body(): intersection = jnp.sum(lax.all_gather(full_intersection, 'sector'), axis=0)  42.3 us
    psum x1, blocking collectives, body(): ham_small = lax.psum(ham_part, ('sector', 'mpo'))  36.9 us
    dot_general x16, matrix products, bond_term(): jnp.einsum('vsac,scd->vsad', left, renv, preferred_element_type=jnp.float32)  29.9 us
    another operation x1, loops' own time, body(): summed = lax.fori_loop(0, lpiece.shape[0], step, empty)  21.2 us
    dynamic_slice x16, local copies, waits for them, and re-layouts, step(): shift = lax.dynamic_index_in_dim(bond_shift, index, 0, keepdims=False)  9.38 us
    ppermute x1, starting transfers between devices, with_halo(): lax.ppermute(tail, axis, [(i, (i + 1) % count) for i in range(ends)])  4.93 us
    dot_general x1, matrix products, body(): jnp.einsum('isab,jsab->ij', vectors, vectors, preferred_element_type=jnp....  4.86 us
    dot_general x1, matrix products, body(): jnp.einsum('isab,jsab->ij', vectors, sigma, preferred_element_type=jnp.fl...  3.64 us
  transfers between devices with their start and end apart: 4, of which 0 were waited for; matrix products, arithmetic and copies ran while one was open for 5% of the time, Pallas kernels for 0%

profile of v1, /device:TPU:0, one launch (start us, length us, event | category | flops | bytes accessed | tf_op | source)
XLA Modules:
  0.0 175.2 jit_solution(11752005464448803224)
XLA Ops:
  7.2 0.7 all-gather.4.cloned.1.call-update
  7.9 0.7 all-gather.6.cloned.1.call-update
  8.7 1.1 constant_dynamic-slice_fusion
  9.9 4.9 %collective-permute-start = (bf16[4,1,256,256]{2,3,0,1:T(8,128)(2,1)S(1)}, bf16[4,1,256,256]{2,3,0,1:T(8,128)(2,1)S(1)}, u32[]{:S(2)}, u32[]{:S(2)}) collective-permute-start(bf16[4,1,256,256]{2,3,0,1:T(8,128)(2,1)S(1)} %copy.27), channel_id=1, source_target_pairs={{0,4},{4,8},{8,12},{12,16},{16,20},{20,24},{24,28},{1,5},{5,9},{9,... | collective-permute-start | bytes 1572872 | tf_op jit(solution)/shard_map/ppermute | solution.py:15
  14.9 1.3 collective-permute-start.1
  16.2 4.9 %fusion.18 = f32[16,16]{1,0:T(8,128)S(1)} fusion(bf16[16,256,256]{2,1,0:T(8,128)(2,1)} %bitcast.57), kind=kOutput, calls=%fused_computation.16 | convolution fusion | flops 33554432 | bytes 2098176 | tf_op jit(solution)/shard_map/isab,jsab->ij/dot_general | solution.py:52
  21.1 42.3 %all-gather = f32[128,16]{1,0:T(8,128)S(1)} all-gather(f32[16,16]{1,0:T(8,128)S(1)} %fusion.18), channel_id=2, replica_groups=mesh['sector'=8,'mpo'=4] {'sector'}, dimensions={0}, use_global_device_ids=true | all-gather | bytes 9216 | tf_op jit(solution)/shard_map/all_gather | solution.py:55
  63.4 0.6 broadcast_multiply_fusion.1
  64.0 0.8 copy-done.1
  64.8 1.4 pad_maximum_fusion
  66.2 60.5 %while.16 = (s32[]{:T(128)}, f32[4,1,256,256]{2,3,0,1:T(8,128)S(1)}, bf16[16,1,256,256]{3,2,1,0:T(8,128)(2,1)}, s32[16]{0:T(128)S(1)}, bf16[4,3,256,256]{2,3,0,1...) while((s32[]{:T(128)}, ...), condition=%wide.region_1.2_spmd.clone, body=%wide.region_0.1_spmd.clone.sunk | while | flops 269221888 | bytes 2884781 | solution.py:46
  66.2 0.6 dynamic_slice.71
  68.1 1.9 %fusion.32 = f32[4,1,256,256]{2,3,0,1:T(8,128)S(1)} fusion(f32[4,1,256,256]{2,3,0,1:T(8,128)S(1)} %get-tuple-element.245, bf16[4,3,256,256]{2,3,0,1:T(8,128)(2,1)S(1)} %get-tuple-element.258, s32[]{:T(128)S(6)} %select_n.28, pred[]{:T(512)S(6)} %compare.3, bf16[16,1,256,256]{3,2,1,0:T(8,128)(2,1)} %get-tuple-element.259, s32[]{:T(128)} %get-tuple-element.244, ...), kind=kOutput, calls=%fused_computation.1.clone.1 | convolution fusion | flops 269221888 | bytes 2884613 | tf_op jit(solution)/shard_map/while/body/eval_jaxpr/vsac,scd->vsad/dot_general | solution.py:29
  70.0 0.6 dynamic_slice.71
  71.9 1.9 %fusion.32 = f32[4,1,256,256]{2,3,0,1:T(8,128)S(1)} fusion(f32[4,1,256,256]{2,3,0,1:T(8,128)S(1)} %get-tuple-element.245, bf16[4,3,256,256]{2,3,0,1:T(8,128)(2,1)S(1)} %get-tuple-element.258, s32[]{:T(128)S(6)} %select_n.28, pred[]{:T(512)S(6)} %compare.3, bf16[16,1,256,256]{3,2,1,0:T(8,128)(2,1)} %get-tuple-element.259, s32[]{:T(128)} %get-tuple-element.244, ...), kind=kOutput, calls=%fused_computation.1.clone.1 | convolution fusion | flops 269221888 | bytes 2884613 | tf_op jit(solution)/shard_map/while/body/eval_jaxpr/vsac,scd->vsad/dot_general | solution.py:29
  75.7 1.9 %fusion.32 = f32[4,1,256,256]{2,3,0,1:T(8,128)S(1)} fusion(f32[4,1,256,256]{2,3,0,1:T(8,128)S(1)} %get-tuple-element.245, bf16[4,3,256,256]{2,3,0,1:T(8,128)(2,1)S(1)} %get-tuple-element.258, s32[]{:T(128)S(6)} %select_n.28, pred[]{:T(512)S(6)} %compare.3, bf16[16,1,256,256]{3,2,1,0:T(8,128)(2,1)} %get-tuple-element.259, s32[]{:T(128)} %get-tuple-element.244, ...), kind=kOutput, calls=%fused_computation.1.clone.1 | convolution fusion | flops 269221888 | bytes 2884613 | tf_op jit(solution)/shard_map/while/body/eval_jaxpr/vsac,scd->vsad/dot_general | solution.py:29
  79.5 1.9 %fusion.32 = f32[4,1,256,256]{2,3,0,1:T(8,128)S(1)} fusion(f32[4,1,256,256]{2,3,0,1:T(8,128)S(1)} %get-tuple-element.245, bf16[4,3,256,256]{2,3,0,1:T(8,128)(2,1)S(1)} %get-tuple-element.258, s32[]{:T(128)S(6)} %select_n.28, pred[]{:T(512)S(6)} %compare.3, bf16[16,1,256,256]{3,2,1,0:T(8,128)(2,1)} %get-tuple-element.259, s32[]{:T(128)} %get-tuple-element.244, ...), kind=kOutput, calls=%fused_computation.1.clone.1 | convolution fusion | flops 269221888 | bytes 2884613 | tf_op jit(solution)/shard_map/while/body/eval_jaxpr/vsac,scd->vsad/dot_general | solution.py:29
  83.2 1.9 %fusion.32 = f32[4,1,256,256]{2,3,0,1:T(8,128)S(1)} fusion(f32[4,1,256,256]{2,3,0,1:T(8,128)S(1)} %get-tuple-element.245, bf16[4,3,256,256]{2,3,0,1:T(8,128)(2,1)S(1)} %get-tuple-element.258, s32[]{:T(128)S(6)} %select_n.28, pred[]{:T(512)S(6)} %compare.3, bf16[16,1,256,256]{3,2,1,0:T(8,128)(2,1)} %get-tuple-element.259, s32[]{:T(128)} %get-tuple-element.244, ...), kind=kOutput, calls=%fused_computation.1.clone.1 | convolution fusion | flops 269221888 | bytes 2884613 | tf_op jit(solution)/shard_map/while/body/eval_jaxpr/vsac,scd->vsad/dot_general | solution.py:29
  87.0 1.9 %fusion.32 = f32[4,1,256,256]{2,3,0,1:T(8,128)S(1)} fusion(f32[4,1,256,256]{2,3,0,1:T(8,128)S(1)} %get-tuple-element.245, bf16[4,3,256,256]{2,3,0,1:T(8,128)(2,1)S(1)} %get-tuple-element.258, s32[]{:T(128)S(6)} %select_n.28, pred[]{:T(512)S(6)} %compare.3, bf16[16,1,256,256]{3,2,1,0:T(8,128)(2,1)} %get-tuple-element.259, s32[]{:T(128)} %get-tuple-element.244, ...), kind=kOutput, calls=%fused_computation.1.clone.1 | convolution fusion | flops 269221888 | bytes 2884613 | tf_op jit(solution)/shard_map/while/body/eval_jaxpr/vsac,scd->vsad/dot_general | solution.py:29
  90.8 1.9 %fusion.32 = f32[4,1,256,256]{2,3,0,1:T(8,128)S(1)} fusion(f32[4,1,256,256]{2,3,0,1:T(8,128)S(1)} %get-tuple-element.245, bf16[4,3,256,256]{2,3,0,1:T(8,128)(2,1)S(1)} %get-tuple-element.258, s32[]{:T(128)S(6)} %select_n.28, pred[]{:T(512)S(6)} %compare.3, bf16[16,1,256,256]{3,2,1,0:T(8,128)(2,1)} %get-tuple-element.259, s32[]{:T(128)} %get-tuple-element.244, ...), kind=kOutput, calls=%fused_computation.1.clone.1 | convolution fusion | flops 269221888 | bytes 2884613 | tf_op jit(solution)/shard_map/while/body/eval_jaxpr/vsac,scd->vsad/dot_general | solution.py:29
  94.6 1.9 %fusion.32 = f32[4,1,256,256]{2,3,0,1:T(8,128)S(1)} fusion(f32[4,1,256,256]{2,3,0,1:T(8,128)S(1)} %get-tuple-element.245, bf16[4,3,256,256]{2,3,0,1:T(8,128)(2,1)S(1)} %get-tuple-element.258, s32[]{:T(128)S(6)} %select_n.28, pred[]{:T(512)S(6)} %compare.3, bf16[16,1,256,256]{3,2,1,0:T(8,128)(2,1)} %get-tuple-element.259, s32[]{:T(128)} %get-tuple-element.244, ...), kind=kOutput, calls=%fused_computation.1.clone.1 | convolution fusion | flops 269221888 | bytes 2884613 | tf_op jit(solution)/shard_map/while/body/eval_jaxpr/vsac,scd->vsad/dot_general | solution.py:29
  98.4 1.9 %fusion.32 = f32[4,1,256,256]{2,3,0,1:T(8,128)S(1)} fusion(f32[4,1,256,256]{2,3,0,1:T(8,128)S(1)} %get-tuple-element.245, bf16[4,3,256,256]{2,3,0,1:T(8,128)(2,1)S(1)} %get-tuple-element.258, s32[]{:T(128)S(6)} %select_n.28, pred[]{:T(512)S(6)} %compare.3, bf16[16,1,256,256]{3,2,1,0:T(8,128)(2,1)} %get-tuple-element.259, s32[]{:T(128)} %get-tuple-element.244, ...), kind=kOutput, calls=%fused_computation.1.clone.1 | convolution fusion | flops 269221888 | bytes 2884613 | tf_op jit(solution)/shard_map/while/body/eval_jaxpr/vsac,scd->vsad/dot_general | solution.py:29
  102.1 1.9 %fusion.32 = f32[4,1,256,256]{2,3,0,1:T(8,128)S(1)} fusion(f32[4,1,256,256]{2,3,0,1:T(8,128)S(1)} %get-tuple-element.245, bf16[4,3,256,256]{2,3,0,1:T(8,128)(2,1)S(1)} %get-tuple-element.258, s32[]{:T(128)S(6)} %select_n.28, pred[]{:T(512)S(6)} %compare.3, bf16[16,1,256,256]{3,2,1,0:T(8,128)(2,1)} %get-tuple-element.259, s32[]{:T(128)} %get-tuple-element.244, ...), kind=kOutput, calls=%fused_computation.1.clone.1 | convolution fusion | flops 269221888 | bytes 2884613 | tf_op jit(solution)/shard_map/while/body/eval_jaxpr/vsac,scd->vsad/dot_general | solution.py:29
  105.9 1.9 %fusion.32 = f32[4,1,256,256]{2,3,0,1:T(8,128)S(1)} fusion(f32[4,1,256,256]{2,3,0,1:T(8,128)S(1)} %get-tuple-element.245, bf16[4,3,256,256]{2,3,0,1:T(8,128)(2,1)S(1)} %get-tuple-element.258, s32[]{:T(128)S(6)} %select_n.28, pred[]{:T(512)S(6)} %compare.3, bf16[16,1,256,256]{3,2,1,0:T(8,128)(2,1)} %get-tuple-element.259, s32[]{:T(128)} %get-tuple-element.244, ...), kind=kOutput, calls=%fused_computation.1.clone.1 | convolution fusion | flops 269221888 | bytes 2884613 | tf_op jit(solution)/shard_map/while/body/eval_jaxpr/vsac,scd->vsad/dot_general | solution.py:29
  109.7 1.9 %fusion.32 = f32[4,1,256,256]{2,3,0,1:T(8,128)S(1)} fusion(f32[4,1,256,256]{2,3,0,1:T(8,128)S(1)} %get-tuple-element.245, bf16[4,3,256,256]{2,3,0,1:T(8,128)(2,1)S(1)} %get-tuple-element.258, s32[]{:T(128)S(6)} %select_n.28, pred[]{:T(512)S(6)} %compare.3, bf16[16,1,256,256]{3,2,1,0:T(8,128)(2,1)} %get-tuple-element.259, s32[]{:T(128)} %get-tuple-element.244, ...), kind=kOutput, calls=%fused_computation.1.clone.1 | convolution fusion | flops 269221888 | bytes 2884613 | tf_op jit(solution)/shard_map/while/body/eval_jaxpr/vsac,scd->vsad/dot_general | solution.py:29
  113.5 1.9 %fusion.32 = f32[4,1,256,256]{2,3,0,1:T(8,128)S(1)} fusion(f32[4,1,256,256]{2,3,0,1:T(8,128)S(1)} %get-tuple-element.245, bf16[4,3,256,256]{2,3,0,1:T(8,128)(2,1)S(1)} %get-tuple-element.258, s32[]{:T(128)S(6)} %select_n.28, pred[]{:T(512)S(6)} %compare.3, bf16[16,1,256,256]{3,2,1,0:T(8,128)(2,1)} %get-tuple-element.259, s32[]{:T(128)} %get-tuple-element.244, ...), kind=kOutput, calls=%fused_computation.1.clone.1 | convolution fusion | flops 269221888 | bytes 2884613 | tf_op jit(solution)/shard_map/while/body/eval_jaxpr/vsac,scd->vsad/dot_general | solution.py:29
  117.3 1.9 %fusion.32 = f32[4,1,256,256]{2,3,0,1:T(8,128)S(1)} fusion(f32[4,1,256,256]{2,3,0,1:T(8,128)S(1)} %get-tuple-element.245, bf16[4,3,256,256]{2,3,0,1:T(8,128)(2,1)S(1)} %get-tuple-element.258, s32[]{:T(128)S(6)} %select_n.28, pred[]{:T(512)S(6)} %compare.3, bf16[16,1,256,256]{3,2,1,0:T(8,128)(2,1)} %get-tuple-element.259, s32[]{:T(128)} %get-tuple-element.244, ...), kind=kOutput, calls=%fused_computation.1.clone.1 | convolution fusion | flops 269221888 | bytes 2884613 | tf_op jit(solution)/shard_map/while/body/eval_jaxpr/vsac,scd->vsad/dot_general | solution.py:29
  121.0 1.9 %fusion.32 = f32[4,1,256,256]{2,3,0,1:T(8,128)S(1)} fusion(f32[4,1,256,256]{2,3,0,1:T(8,128)S(1)} %get-tuple-element.245, bf16[4,3,256,256]{2,3,0,1:T(8,128)(2,1)S(1)} %get-tuple-element.258, s32[]{:T(128)S(6)} %select_n.28, pred[]{:T(512)S(6)} %compare.3, bf16[16,1,256,256]{3,2,1,0:T(8,128)(2,1)} %get-tuple-element.259, s32[]{:T(128)} %get-tuple-element.244, ...), kind=kOutput, calls=%fused_computation.1.clone.1 | convolution fusion | flops 269221888 | bytes 2884613 | tf_op jit(solution)/shard_map/while/body/eval_jaxpr/vsac,scd->vsad/dot_general | solution.py:29
  124.8 1.9 %fusion.32 = f32[4,1,256,256]{2,3,0,1:T(8,128)S(1)} fusion(f32[4,1,256,256]{2,3,0,1:T(8,128)S(1)} %get-tuple-element.245, bf16[4,3,256,256]{2,3,0,1:T(8,128)(2,1)S(1)} %get-tuple-element.258, s32[]{:T(128)S(6)} %select_n.28, pred[]{:T(512)S(6)} %compare.3, bf16[16,1,256,256]{3,2,1,0:T(8,128)(2,1)} %get-tuple-element.259, s32[]{:T(128)} %get-tuple-element.244, ...), kind=kOutput, calls=%fused_computation.1.clone.1 | convolution fusion | flops 269221888 | bytes 2884613 | tf_op jit(solution)/shard_map/while/body/eval_jaxpr/vsac,scd->vsad/dot_general | solution.py:29
  126.9 3.6 %fusion.21 = f32[16,4]{0,1:T(4,128)S(1)} fusion(bf16[16,256,256]{2,1,0:T(8,128)(2,1)} %bitcast.58, bf16[4,256,256]{2,1,0:T(8,128)(2,1)S(1)} %bitcast.55), kind=kOutput, calls=%fused_computation.17 | convolution fusion | flops 8388608 | bytes 2621696 | tf_op jit(solution)/shard_map/isab,jsab->ij/dot_general | solution.py:50
  130.8 36.9 %psum.7 = f32[16,16]{1,0:T(8,128)S(1)} all-reduce(f32[16,16]{1,0:T(8,128)S(1)} %dynamic_update_slice.3), channel_id=1, replica_groups=mesh['sector'=8,'mpo'=4] {'sector','mpo'}, use_global_device_ids=true, to_apply=%region_3.4 | all-reduce | flops 256 | bytes 2048 | tf_op jit(solution)/shard_map/psum | solution.py:56
  167.7 0.6 broadcast_multiply_fusion
  (32 shorter events, 9.0 us)
Async XLA Ops:
  7.2 59.0 %all-gather.4.cloned.1.call-start = ((), (), s32[]{:S(2)}) async-start(), calls=%async_computation | async-start | bytes 2621440 | tf_op jit(solution)/shard_map/all_gather | solution.py:40
  7.9 58.3 %all-gather.6.cloned.1.call-start = ((), (), s32[]{:S(2)}) async-start(), calls=%async_computation.1 | async-start | bytes 2621440 | tf_op jit(solution)/shard_map/all_gather | solution.py:39
  9.9 54.0 %collective-permute-start = (bf16[4,1,256,256]{2,3,0,1:T(8,128)(2,1)S(1)}, bf16[4,1,256,256]{2,3,0,1:T(8,128)(2,1)S(1)}, u32[]{:S(2)}, u32[]{:S(2)}) collective-permute-start(bf16[4,1,256,256]{2,3,0,1:T(8,128)(2,1)S(1)} %copy.27), channel_id=1, source_target_pairs={{0,4},{4,8},{8,12},{12,16},{16,20},{20,24},{24,28},{1,5},{5,9},{9,... | collective-permute-start | bytes 1572872 | tf_op jit(solution)/shard_map/ppermute | solution.py:15
  14.9 49.9 %collective-permute-start.1 = (bf16[4,1,256,256]{2,3,0,1:T(8,128)(2,1)S(1)}, bf16[4,1,256,256]{2,3,0,1:T(8,128)(2,1)}, u32[]{:S(2)}, u32[]{:S(2)}) collective-permute-start(bf16[4,1,256,256]{2,3,0,1:T(8,128)(2,1)S(1)} %copy.27), channel_id=1, source_target_pairs={{4,0},{8,4},{12,8},{16,12},{20,16},{24,20},{28,24},{5,1},{9,5},{13... | collective-permute-start | bytes 1572872 | tf_op jit(solution)/shard_map/ppermute | solution.py:17
  21.1 45.2 %copy-start.2 = (s32[16]{0:T(128)S(1)}, s32[16]{0:T(128)}, u32[]{:S(2)}) copy-start(s32[16]{0:T(128)} %param.9) | copy-start | bytes 196
  64.0 0.8 copy-start.1
  126.9 41.4 %copy-start = (bf16[4,1,256,256]{3,2,1,0:T(8,128)(2,1)}, bf16[4,1,256,256]{3,2,1,0:T(8,128)(2,1)S(1)}, u32[]{:S(2)}) copy-start(bf16[4,1,256,256]{3,2,1,0:T(8,128)(2,1)S(1)} %copy.19) | copy-start | bytes 1572868
Sparse Core Ops, SparseCore 0:
  9.5 25.2 all-gather.3
  36.4 22.5 all-gather.5
